TPU v7x, 32 devices: a whole 2x2x4 slice. The times are simulated.
32 devices in a mesh: row: 4 (over z), col: 8 (over y, x, core).
Axes of the slice: x: 2, y: 2, z: 4, core: 2. Of those that a mesh axis runs over, the one named last changes fastest.
Arguments:
- front: float32 [8192, 8192], P('row', 'col'), may hold values from -6 to 6
- inverses: float32 [2, 512, 512], replicated, may hold values from -2 to 2, as said below
- block_owner: int32 [64, 64], P('row', 'col'), may hold values from -1 to 31, as said below
- block_slot: int32 [64, 64], P('row', 'col'), may hold values from 0 to 47
- parent_in: float32 [1536, 128, 128], P(('row', 'col')), may hold values from -6 to 6
Outputs:
- updated: float32 [8192, 8192], P('row', 'col')
- panels: float32 [8192, 1024], P(('row', 'col'))
- parent_out: float32 [1536, 128, 128], P(('row', 'col'))
Inputs may be any that keep to these rules, and one draw needn't show every extreme that they name: Entries of the pivot block inverses. `block_owner`: -1 exactly for blocks above the diagonal (I < J); on one device's 16 x 8 blocks no device is named more than 4 times, and on some device some device is named exactly 4 times.
All inputs are finite; a program needn't handle non-finite values.
Results may differ from a plain program's by a relative error of at most 0.00014.
Values sent between devices are 32-bit elements; how exact they have to be, the bound alone decides.
A program may use at most 128 MiB of HBM per device.

v0:
```python
import jax
import jax.numpy as jnp
from jax import lax
from jax.sharding import PartitionSpec as P


def spread_2(block, axis, source):
    block = jnp.where(lax.axis_index(axis) == source, block, jnp.zeros_like(block))
    return lax.psum(block, axis)


def matmul(left_side, right_side):
    return jnp.dot(
        left_side, right_side, preferred_element_type=jnp.float32, precision=lax.Precision.HIGHEST
    )


def spread(columns, rows):
    columns = spread_2(columns, "col", 0)
    rows = spread_2(rows, "row", 0)
    return (columns, rows)


def local(front, inverses, block_owner, block_slot, parent_in):
    panel_width = inverses.shape[1]
    columns_one, rows_one = spread(front[:, 0:panel_width], front[0:panel_width, :])
    factor_one = matmul(columns_one, inverses[0])
    partial_value = front - matmul(factor_one, rows_one)
    columns_two, rows_two = spread(
        partial_value[:, panel_width : 2 * panel_width],
        partial_value[panel_width : 2 * panel_width, :],
    )
    factor_two = matmul(columns_two, inverses[1])
    factors = jnp.concatenate([factor_one, factor_two], axis=1)
    updated = partial_value - matmul(factor_two, rows_two)
    piece_rows = factors.shape[0] // lax.axis_size("col")
    panels = lax.dynamic_slice_in_dim(factors, lax.axis_index("col") * piece_rows, piece_rows, 0)
    block_rows, block_cols = block_owner.shape
    block_edge = parent_in.shape[1]
    held = parent_in.shape[0]
    block_count = block_rows * block_cols
    row_devices = lax.axis_size("row")
    col_devices = lax.axis_size("col")
    devices = row_devices * col_devices
    capacity = max(1, (block_count + devices - 1) // devices)
    blocks = updated.reshape(block_rows, block_edge, block_cols, block_edge).transpose(0, 2, 1, 3)
    blocks = blocks.reshape(block_count, block_edge, block_edge)
    owners = block_owner.reshape(block_count)
    parent_slots = block_slot.reshape(block_count)
    position = jnp.arange(block_count, dtype=jnp.int32)
    earlier = (owners[:, None] == owners[None, :]) & (position[None, :] < position[:, None])
    within = jnp.sum(earlier.astype(jnp.int32), axis=1)
    target = jnp.where(owners >= 0, owners * capacity + within, devices * capacity)
    outgoing = (
        jnp.zeros((devices * capacity, block_edge, block_edge), jnp.float32)
        .at[target]
        .set(blocks, mode="drop")
    )
    labels = (
        jnp.full((devices * capacity,), held, jnp.float32)
        .at[target]
        .set(parent_slots.astype(jnp.float32), mode="drop")
    )
    arrived, markers = (
        lax.all_to_all(
            outgoing.reshape(devices, capacity, block_edge, block_edge),
            ("row", "col"),
            split_axis=0,
            concat_axis=0,
            tiled=True,
        ),
        lax.all_to_all(
            labels.reshape(devices, capacity),
            ("row", "col"),
            split_axis=0,
            concat_axis=0,
            tiled=True,
        ),
    )
    arrived = arrived.reshape(devices * capacity, block_edge, block_edge)
    markers = markers.reshape(devices * capacity).astype(jnp.int32)
    added = jnp.zeros(parent_in.shape, jnp.float32).at[markers].add(arrived, mode="drop")
    parent_out = parent_in + added
    return (updated, panels, parent_out)


def solution(mesh):
    in_specs = (
        P("row", "col"),
        P(),
        P("row", "col"),
        P("row", "col"),
        P(("row", "col"), None, None),
    )
    out_specs = (P("row", "col"), P(("row", "col"), None), P(("row", "col"), None, None))
    return jax.shard_map(local, mesh=mesh, in_specs=in_specs, out_specs=out_specs, check_vma=False)
```

profile of v0, /device:TPU:0, one launch (start us, length us, event | category | flops | bytes accessed | tf_op | source)
XLA Modules:
  0.0 644.3 jit_solution(14133104792628374288)
XLA Ops:
  7.2 4.7 slice_select_fusion.1
  12.0 3.3 slice_select_fusion.3
  15.4 80.2 %all-reduce.5.cloned.1.call-done = f32[2048,512]{1,0:T(8,128)} async-done(((f32[2048,512]{1,0:T(8,128)}), f32[2048,512]{1,0:T(8,128)}) %all-reduce.5.cloned.1.call-update) | async-done | bytes 4194320 | tf_op jit(solution)/shard_map/psum | solution.py:9
  95.6 10.0 %fusion.3 = f32[2048,512]{0,1:T(8,128)} fusion(f32[2048,512]{1,0:T(8,128)} %all-reduce.5.cloned.1.call-done, f32[2,512,512]{2,1,0:T(8,128)S(1)} %copy-done.4), kind=kOutput, calls=%fused_computation.14 | convolution fusion | flops 6442450944 | bytes 9437184 | tf_op jit(solution)/shard_map/dot_general | solution.py:13
  105.6 79.2 %all-reduce.7.cloned.1.call-done = f32[512,1024]{1,0:T(8,128)} async-done(((f32[512,1024]{1,0:T(8,128)}), f32[512,1024]{1,0:T(8,128)}) %all-reduce.7.cloned.1.call-update) | async-done | bytes 2097168 | tf_op jit(solution)/shard_map/psum | solution.py:9
  184.8 16.6 %convolution_subtract_fusion.1 = f32[2048,1024]{1,0:T(8,128)S(1)} fusion(f32[2048,1024]{1,0:T(8,128)} %param.5, f32[2048,512]{0,1:T(8,128)} %fusion.3, f32[512,1024]{1,0:T(8,128)} %all-reduce.7.cloned.1.call-done), kind=kOutput, calls=%fused_computation.8 | convolution fusion | flops 12886999040 | bytes 23068672 | tf_op jit(solution)/shard_map/dot_general | solution.py:13
  201.4 3.4 copy-done
  204.8 2.7 slice_select_fusion
  207.6 3.2 slice_select_fusion.2
  213.4 3.8 all-to-all-start
  217.2 70.5 %all-reduce.9.cloned.1.call-done = f32[2048,512]{1,0:T(8,128)} async-done(((f32[2048,512]{1,0:T(8,128)}), f32[2048,512]{1,0:T(8,128)}) %all-reduce.9.cloned.1.call-update) | async-done | bytes 4194320 | tf_op jit(solution)/shard_map/psum | solution.py:9
  287.8 10.0 %fusion.1 = f32[2048,512]{0,1:T(8,128)} fusion(f32[2048,512]{1,0:T(8,128)} %all-reduce.9.cloned.1.call-done, f32[2,512,512]{2,1,0:T(8,128)S(1)} %copy-done.4), kind=kOutput, calls=%fused_computation.12 | convolution fusion | flops 6442450944 | bytes 9437184 | tf_op jit(solution)/shard_map/dot_general | solution.py:13
  297.7 79.1 %all-reduce.11.cloned.1.call-done = f32[512,1024]{1,0:T(8,128)} async-done(((f32[512,1024]{1,0:T(8,128)}), f32[512,1024]{1,0:T(8,128)}) %all-reduce.11.cloned.1.call-update) | async-done | bytes 2097168 | tf_op jit(solution)/shard_map/psum | solution.py:9
  376.8 16.8 %convolution_subtract_fusion = f32[2048,1024]{1,0:T(8,128)S(1)} fusion(f32[2048,1024]{1,0:T(8,128)} %copy-done, f32[2048,512]{0,1:T(8,128)} %fusion.1, f32[512,1024]{1,0:T(8,128)} %all-reduce.11.cloned.1.call-done), kind=kOutput, calls=%fused_computation.7 | convolution fusion | flops 12886999040 | bytes 23068672 | tf_op jit(solution)/shard_map/dot_general | solution.py:13
  393.6 2.2 copy.33
  397.3 4.7 copy.31
  402.0 4.3 broadcast_in_dim.18
  406.3 23.0 %scatter_fusion = f32[128,128,128]{2,1,0:T(8,128)} fusion(f32[128,128,128]{2,1,0:T(8,128)} %broadcast_in_dim.18, s32[128]{0:T(128)S(1)} %fusion.8, f32[128,128,128]{2,1,0:T(8,128)} %bitcast.35), kind=kCustom, calls=%fused_computation.1 | custom fusion | bytes 25166336 | tf_op jit(solution)/shard_map/scatter | solution.py:57
  429.3 3.8 all-to-all-start.1
  433.3 2.4 fusion
  435.7 2.5 copy.32
  438.2 180.8 %all-to-all-done.1 = f32[32,4,128,128]{3,2,1,0:T(8,128)} async-done(((f32[32,4,128,128]{3,2,1,0:T(8,128)}), f32[32,4,128,128]{3,2,1,0:T(8,128)}, u32[]{:S(2)}, u32[]{:S(2)}) %all-to-all-start.1) | async-done | bytes 8388640 | tf_op jit(solution)/shard_map/all_to_all | solution.py:65
  619.0 17.0 %scatter_fusion.1 = f32[48,128,128]{2,1,0:T(8,128)S(1)} fusion(f32[48,128,128]{2,1,0:T(8,128)S(1)} %copy-done.2, s32[128]{0:T(128)S(1)} %fusion.9, f32[128,128,128]{2,1,0:T(8,128)} %bitcast.9), kind=kCustom, calls=%fused_computation.2 | custom fusion | flops 2097152 | bytes 25166336 | tf_op jit(solution)/shard_map/scatter-add | solution.py:82
  636.1 1.7 copy-done.1
  (39 shorter events, 4.5 us)
Async XLA Ops:
  7.2 88.5 %all-reduce.5.cloned.1.call-start = ((), (), s32[]{:S(2)}) async-start(), calls=%async_computation.2 | async-start | bytes 8388608 | tf_op jit(solution)/shard_map/psum | solution.py:9
  11.9 83.7 %copy-start.4 = (f32[2,512,512]{2,1,0:T(8,128)S(1)}, f32[2,512,512]{2,1,0:T(8,128)}, u32[]{:S(2)}) copy-start(f32[2,512,512]{2,1,0:T(8,128)} %param.6) | copy-start | bytes 6291460
  12.0 172.8 %all-reduce.7.cloned.1.call-start = ((), (), s32[]{:S(2)}) async-start(), calls=%async_computation.3 | async-start | bytes 4194304 | tf_op jit(solution)/shard_map/psum | solution.py:9
  15.4 272.4 %all-reduce.9.cloned.1.call-start = ((), (), s32[]{:S(2)}) async-start(), calls=%async_computation.4 | async-start | bytes 8388608 | tf_op jit(solution)/shard_map/psum | solution.py:9
  201.4 3.4 copy-start
  207.5 3.3 copy-start.5
  207.5 3.6 copy-start.6
  207.5 169.3 %all-reduce.11.cloned.1.call-start = ((), (), s32[]{:S(2)}) async-start(), calls=%async_computation.5 | async-start | bytes 4194304 | tf_op jit(solution)/shard_map/psum | solution.py:9
  213.4 215.9 %all-to-all-start = ((f32[32,1,4]{2,1,0:T(1,128)}), f32[32,1,4]{2,1,0:T(1,128)S(1)}, u32[]{:S(2)}, u32[]{:S(2)}) async-start(f32[32,1,4]{2,1,0:T(1,128)} %bitcast.4), calls=%async_computation | async-start | bytes 32768 | tf_op jit(solution)/shard_map/all_to_all | solution.py:72
  393.6 3.7 copy-start.3
  429.3 189.7 %all-to-all-start.1 = ((f32[32,4,128,128]{3,2,1,0:T(8,128)}), f32[32,4,128,128]{3,2,1,0:T(8,128)}, u32[]{:S(2)}, u32[]{:S(2)}) async-start(f32[32,4,128,128]{3,2,1,0:T(8,128)} %bitcast.33), calls=%async_computation.1 | async-start | bytes 16777216 | tf_op jit(solution)/shard_map/all_to_all | solution.py:65
  433.3 185.7 %copy-start.2 = (f32[48,128,128]{2,1,0:T(8,128)S(1)}, f32[48,128,128]{2,1,0:T(8,128)}, u32[]{:S(2)}) copy-start(f32[48,128,128]{2,1,0:T(8,128)} %param.9) | copy-start | bytes 9437188
  636.1 1.7 copy-start.1
Sparse Core Ops, SparseCore 0:
  12.1 83.5 all-reduce.4
  98.6 86.1 all-reduce.6
  207.6 80.1 all-reduce.8
  290.6 86.1 all-reduce.10
where the time goes:
time: 645 us; the launch traced here: 644 us
  waiting for transfers between devices  490 us (76%)
  matrix products  53.3 us (8%)
  local copies, waits for them, and re-layouts  45.8 us (7%)
  other arithmetic  33.6 us (5%)
  between operations  14 us (2%)
  starting transfers between devices  7.79 us (1%)
    psum x4, waiting for transfers between devices, spread_2(): return lax.psum(block, axis)  309 us
    all_to_all x1, waiting for transfers between devices, local(): lax.all_to_all(outgoing.reshape(devices, capacity, block_edge, block_edge...  181 us
    dot_general x4, matrix products, matmul(): jnp.dot(left_side, right_side, preferred_element_type=jnp.float32, precis...  53.3 us
    scatter x1, local copies, waits for them, and re-layouts, local(): outgoing = jnp.zeros((devices * capacity, block_edge, block_edge), jnp.fl...  23 us
    scatter-add x1, other arithmetic, local(): jnp.zeros(parent_in.shape, jnp.float32).at[markers]  17 us
    select_n x4, other arithmetic, spread_2(): jnp.where(lax.axis_index(axis) == source, block, jnp.zeros_like(block))  13.9 us
  transfers between devices with their start and end apart: 6, of which 5 were waited for; matrix products, arithmetic and copies ran while one was open for 13% of the time, Pallas kernels for 0%

commit v1 on v0

--- a/solution.py
+++ b/solution.py
@@ -6,7 +6,7 @@
 
 def spread_2(block, axis, source):
     block = jnp.where(lax.axis_index(axis) == source, block, jnp.zeros_like(block))
-    return lax.psum(block, axis)
+    return jnp.sum(lax.all_gather(block, axis), axis=0)
 
 
 def matmul(left_side, right_side):

time: 645 us -> 978 us (1.52)
  waiting for transfers between devices: 490 us -> 779 us
  other arithmetic: 33.6 us -> 73.2 us
    all_gather x0 -> x4, waiting for transfers between devices: none -> 598 us  [spread_2(): return jnp.sum(lax.all_gather(block, axis), axis=0)]
    psum x4 -> x0, waiting for transfers between devices: 309 us -> none  [spread_2(): return lax.psum(block, axis)]
    reduce_sum x0 -> x4, other arithmetic: none -> 39.5 us  [spread_2(): return jnp.sum(lax.all_gather(block, axis), axis=0)]
  transfers between devices with their start and end apart: 6 -> 6, of which waited for: 5 -> 5; matrix products, arithmetic and copies ran while one was open for 13% -> 10% of each run, Pallas kernels for 0% -> 0%
where the time goes in v1:
time: 978 us; the launch traced here: 977 us
  waiting for transfers between devices  779 us (80%)
  other arithmetic  73.2 us (7%)
  matrix products  55.1 us (6%)
  local copies, waits for them, and re-layouts  46.6 us (5%)
  between operations  14 us (1%)
    all_gather x4, waiting for transfers between devices, spread_2(): return jnp.sum(lax.all_gather(block, axis), axis=0)  598 us
    all_to_all x1, waiting for transfers between devices, local(): lax.all_to_all(outgoing.reshape(devices, capacity, block_edge, block_edge...  181 us
    dot_general x4, matrix products, matmul(): jnp.dot(left_side, right_side, preferred_element_type=jnp.float32, precis...  55.1 us
    reduce_sum x4, other arithmetic, spread_2(): return jnp.sum(lax.all_gather(block, axis), axis=0)  39.5 us
    scatter x1, local copies, waits for them, and re-layouts, local(): outgoing = jnp.zeros((devices * capacity, block_edge, block_edge), jnp.fl...  23 us
  transfers between devices with their start and end apart: 6, of which 5 were waited for; matrix products, arithmetic and copies ran while one was open for 10% of the time, Pallas kernels for 0%

profile of v1, /device:TPU:0, one launch (start us, length us, event | category | flops | bytes accessed | tf_op | source)
XLA Modules:
  0.0 977.2 jit_solution(14333292316742326603)
XLA Ops:
  7.2 3.2 slice_select_fusion.3
  10.5 4.7 slice_select_fusion.1
  15.3 147.7 %all-gather.11.cloned.1.call-done = f32[2048,1024]{1,0:T(8,128)} async-done(((f32[512,1024]{1,0:T(8,128)}), f32[2048,1024]{1,0:T(8,128)}) %all-gather.11.cloned.1.call-update) | async-done | bytes 8388624 | tf_op jit(solution)/shard_map/all_gather | solution.py:9
  162.9 4.6 reduce_sum.48
  167.5 156.8 %all-gather.9.cloned.1.call-done = f32[16384,512]{1,0:T(8,128)} async-done(((f32[2048,512]{1,0:T(8,128)}), f32[16384,512]{1,0:T(8,128)}) %all-gather.9.cloned.1.call-update) | async-done | bytes 33554448 | tf_op jit(solution)/shard_map/all_gather | solution.py:9
  324.3 15.2 %reduce_sum.47 = f32[2048,512]{1,0:T(8,128)} reduce(f32[8,2048,512]{2,1,0:T(8,128)} %bitcast.38, f32[]{:T(128)} %constant.12.clone.1), dimensions={0}, to_apply=%region_0.1 | reduce | flops 7340032 | bytes 37748740 | tf_op jit(solution)/shard_map/reduce_sum | solution.py:9
  339.5 8.9 fusion.3
  348.5 18.5 %convolution_subtract_fusion.1 = f32[2048,1024]{1,0:T(8,128)S(1)} fusion(f32[2048,1024]{1,0:T(8,128)} %param.5, f32[2048,512]{0,1:T(8,128)S(1)} %fusion.3, f32[512,1024]{1,0:T(8,128)S(1)} %reduce_sum.48), kind=kOutput, calls=%fused_computation.8 | convolution fusion | flops 12886999040 | bytes 23068672 | tf_op jit(solution)/shard_map/dot_general | solution.py:13
  367.0 3.4 copy-done
  372.0 4.6 slice_select_fusion
  380.2 4.6 all-to-all-start
  384.8 137.3 %all-gather.15.cloned.1.call-done = f32[2048,1024]{1,0:T(8,128)} async-done(((f32[512,1024]{1,0:T(8,128)}), f32[2048,1024]{1,0:T(8,128)}) %all-gather.15.cloned.1.call-update) | async-done | bytes 8388624 | tf_op jit(solution)/shard_map/all_gather | solution.py:9
  522.1 4.6 reduce_sum.50
  526.7 156.0 %all-gather.13.cloned.1.call-done = f32[16384,512]{1,0:T(8,128)} async-done(((f32[2048,512]{1,0:T(8,128)}), f32[16384,512]{1,0:T(8,128)}) %all-gather.13.cloned.1.call-update) | async-done | bytes 33554448 | tf_op jit(solution)/shard_map/all_gather | solution.py:9
  682.7 15.1 %reduce_sum.49 = f32[2048,512]{1,0:T(8,128)} reduce(f32[8,2048,512]{2,1,0:T(8,128)} %bitcast.37, f32[]{:T(128)} %constant.12.clone.1), dimensions={0}, to_apply=%region_2.3 | reduce | flops 7340032 | bytes 37748740 | tf_op jit(solution)/shard_map/reduce_sum | solution.py:9
  697.8 8.9 fusion.1
  706.8 18.6 %convolution_subtract_fusion = f32[2048,1024]{1,0:T(8,128)S(1)} fusion(f32[2048,1024]{1,0:T(8,128)} %copy-done, f32[2048,512]{0,1:T(8,128)S(1)} %fusion.1, f32[512,1024]{1,0:T(8,128)S(1)} %reduce_sum.50), kind=kOutput, calls=%fused_computation.7 | convolution fusion | flops 12886999040 | bytes 23068672 | tf_op jit(solution)/shard_map/dot_general | solution.py:13
  729.2 4.7 copy.31
  733.8 4.3 broadcast_in_dim.18
  738.1 23.0 %scatter_fusion = f32[128,128,128]{2,1,0:T(8,128)} fusion(f32[128,128,128]{2,1,0:T(8,128)} %broadcast_in_dim.18, s32[128]{0:T(128)S(1)} %fusion.8, f32[128,128,128]{2,1,0:T(8,128)} %bitcast.39), kind=kCustom, calls=%fused_computation.1 | custom fusion | bytes 25166336 | tf_op jit(solution)/shard_map/scatter | solution.py:57
  761.1 5.0 all-to-all-start.1
  768.7 2.5 copy.32
  771.2 180.8 %all-to-all-done.1 = f32[32,4,128,128]{3,2,1,0:T(8,128)} async-done(((f32[32,4,128,128]{3,2,1,0:T(8,128)}), f32[32,4,128,128]{3,2,1,0:T(8,128)}, u32[]{:S(2)}, u32[]{:S(2)}) %all-to-all-start.1) | async-done | bytes 8388640 | tf_op jit(solution)/shard_map/all_to_all | solution.py:65
  952.0 17.0 %scatter_fusion.1 = f32[48,128,128]{2,1,0:T(8,128)S(1)} fusion(f32[48,128,128]{2,1,0:T(8,128)S(1)} %copy-done.4, s32[128]{0:T(128)S(1)} %fusion.9, f32[128,128,128]{2,1,0:T(8,128)} %bitcast.13), kind=kCustom, calls=%fused_computation.2 | custom fusion | flops 2097152 | bytes 25166336 | tf_op jit(solution)/shard_map/scatter-add | solution.py:82
  (45 shorter events, 13.2 us)
Async XLA Ops:
  7.2 155.8 %all-gather.11.cloned.1.call-start = ((), (), s32[]{:S(2)}) async-start(), calls=%async_computation.3 | async-start | bytes 10485760 | tf_op jit(solution)/shard_map/all_gather | solution.py:9
  10.4 313.8 %all-gather.9.cloned.1.call-start = ((), (), s32[]{:S(2)}) async-start(), calls=%async_computation.2 | async-start | bytes 37748736 | tf_op jit(solution)/shard_map/all_gather | solution.py:9
  15.2 506.9 %all-gather.15.cloned.1.call-start = ((), (), s32[]{:S(2)}) async-start(), calls=%async_computation.5 | async-start | bytes 10485760 | tf_op jit(solution)/shard_map/all_gather | solution.py:9
  348.5 18.6 %copy-start.1 = (f32[2048,512]{0,1:T(8,128)}, f32[2048,512]{0,1:T(8,128)S(1)}, u32[]{:S(2)}) copy-start(f32[2048,512]{0,1:T(8,128)S(1)} %fusion.3) | copy-start | bytes 12582916
  367.0 3.4 copy-start
  372.0 310.7 %all-gather.13.cloned.1.call-start = ((), (), s32[]{:S(2)}) async-start(), calls=%async_computation.4 | async-start | bytes 37748736 | tf_op jit(solution)/shard_map/all_gather | solution.py:9
  376.7 0.7 copy-start.6
  376.7 1.2 copy-start.7
  380.2 380.9 %all-to-all-start = ((f32[32,1,4]{2,1,0:T(1,128)}), f32[32,1,4]{2,1,0:T(1,128)S(1)}, u32[]{:S(2)}, u32[]{:S(2)}) async-start(f32[32,1,4]{2,1,0:T(1,128)} %bitcast.8), calls=%async_computation | async-start | bytes 32768 | tf_op jit(solution)/shard_map/all_to_all | solution.py:72
  706.7 18.7 %copy-start.2 = (f32[2048,512]{0,1:T(8,128)}, f32[2048,512]{0,1:T(8,128)S(1)}, u32[]{:S(2)}) copy-start(f32[2048,512]{0,1:T(8,128)S(1)} %fusion.1) | copy-start | bytes 12582916
  725.4 3.7 copy-start.5
  761.1 190.9 %all-to-all-start.1 = ((f32[32,4,128,128]{3,2,1,0:T(8,128)}), f32[32,4,128,128]{3,2,1,0:T(8,128)}, u32[]{:S(2)}, u32[]{:S(2)}) async-start(f32[32,4,128,128]{3,2,1,0:T(8,128)} %bitcast.35), calls=%async_computation.1 | async-start | bytes 16777216 | tf_op jit(solution)/shard_map/all_to_all | solution.py:65
  766.3 185.7 %copy-start.4 = (f32[48,128,128]{2,1,0:T(8,128)S(1)}, f32[48,128,128]{2,1,0:T(8,128)}, u32[]{:S(2)}) copy-start(f32[48,128,128]{2,1,0:T(8,128)} %param.9) | copy-start | bytes 9437188
  969.0 1.7 copy-start.3
Sparse Core Ops, SparseCore 0:
  10.6 152.3 all-gather.10
  165.4 158.8 all-gather.8
  372.1 149.9 all-gather.14
  523.8 158.8 all-gather.12
